TPU v7x, 768 devices: a whole 4x8x12 slice. The times are simulated.
768 devices in a mesh: blk: 96 (over x, y, z_hi), lane: 8 (over z_lo, core).
Axes of the slice: x: 4, y: 8, z: 12 (z_hi: 3, z_lo: 4; z = z_hi * 4 + z_lo), core: 2. Of those that a mesh axis runs over, the one named last changes fastest.
Arguments:
- points: bfloat16 [786432, 128], P(('blk', 'lane')), may hold values from -6 to 6
- probes: bfloat16 [786432, 128], P(('blk', 'lane')), may hold values from -6 to 6
- inv_scale: float32 [128], replicated, may hold values from 0.02 to 0.5
- noise_var: float32 [1], replicated, may hold values from 0.1 to 1
Outputs:
- product: float32 [786432, 128], P(('blk', 'lane'))
All inputs are finite; a program needn't handle non-finite values.
Results may differ from a plain program's by a relative error of at most 0.0003.
Values may be sent and summed in bfloat16 or wider, within the bound.
A program may use at most 32 MiB of HBM per device.

v0:
```python
import functools
import math

import jax
import jax.numpy as jnp
from jax import lax
from jax.experimental import pallas as pl
from jax.experimental.pallas import tpu as pltpu
from jax.sharding import PartitionSpec as P

MESH = pl.DeviceIdType.MESH
LOG2E = math.log2(math.e)
LN2 = math.log(2.0)
SHIFT = math.log2(LN2 * LN2 / 3.0)
LIN = 3.0 / LN2
CON = 3.0 / (LN2 * LN2)
ROWS = 512
COLS = 256
COMPUTE = True
COMM = True

OWN, PARTNER, LEFT, RIGHT, PLEFT, PRIGHT, FAR = range(7)


def matern(minus_cross, own_sq, other_sq):
    x = jnp.maximum(minus_cross + own_sq + other_sq, 1e-30)
    u = x * lax.rsqrt(x)
    return jnp.exp2(SHIFT - u) * (u * (u + LIN) + CON)


def split(x, parts):
    out = []
    for _ in range(parts):
        piece = x.astype(jnp.bfloat16)
        out.append(piece)
        x = x - piece.astype(jnp.float32)
    return out


def kernel(n_lane, n_dev, p_hbm, v_hbm, scale_ref, noise_ref, o_ref,
           buf, norms, own_sq, left, acc, load_sem, send_sem, recv_sem, nsend_sem, nrecv_sem):
    pts = p_hbm.shape[0]
    n_piece = pts // ROWS
    me = lax.axis_index("blk") * n_lane + lax.axis_index("lane")
    core = lax.rem(me, 2)

    def device(step):
        there = lax.rem(me + step + n_dev, n_dev)
        return (there // n_lane, lax.rem(there, n_lane))

    partner, outer = device(1 - 2 * core), device(2 * core - 1)
    lower, upper = device(-2), device(2)

    loads = [pltpu.make_async_copy(p_hbm, buf.at[OWN, 0], load_sem.at[0]),
             pltpu.make_async_copy(v_hbm, buf.at[OWN, 1], load_sem.at[1])]
    for load in loads:
        load.start()
    if COMM:
        barrier = pltpu.get_barrier_semaphore()
        for there in (partner, outer, lower, upper):
            pl.semaphore_signal(barrier, inc=1, device_id=there, device_id_type=MESH)

    loads[0].wait()
    gain = scale_ref[...] * (math.sqrt(5.0) * LOG2E)
    gain = gain * gain
    ones = jnp.ones((8, 384), jnp.bfloat16)
    for j in range(0, pts, 256):
        p = buf[OWN, 0, j:j + 256, :].astype(jnp.float32)
        hi, lo = split(-2.0 * (p * gain), 2)
        left[j:j + 256, 0:128] = hi
        left[j:j + 256, 128:256] = lo
        q = p * (-0.5 * (hi.astype(jnp.float32) + lo.astype(jnp.float32)))
        row = lax.dot_general(ones, jnp.concatenate(split(q, 3), axis=1), (((1,), (1,)), ((), ())),
                              preferred_element_type=jnp.float32)
        own_sq[:, j:j + 256] = row
        norms[OWN, j // 128:j // 128 + 1, :] = row[0:1, 0:128]
        norms[OWN, j // 128 + 1:j // 128 + 2, :] = row[0:1, 128:256]
    loads[1].wait()

    sent = []

    def send(lane_no, src, dst, piece, there):
        for k in range(2):
            rows = pl.ds(piece * ROWS, ROWS)
            c = pltpu.make_async_remote_copy(
                buf.at[src, k, rows], buf.at[dst, k, rows], send_sem.at[lane_no, piece, k],
                recv_sem.at[dst, piece, k], device_id=there, device_id_type=MESH)
            c.start()
            sent.append(c)

    def send_norm(lane_no, src, dst, there):
        c = pltpu.make_async_remote_copy(
            norms.at[src], norms.at[dst], nsend_sem.at[lane_no], nrecv_sem.at[dst],
            device_id=there, device_id_type=MESH)
        c.start()
        sent.append(c)

    def arrived(slot, piece):
        for k in range(2):
            rows = pl.ds(piece * ROWS, ROWS)
            pltpu.make_async_remote_copy(
                buf.at[slot, k, rows], buf.at[slot, k, rows], send_sem.at[0, 0, 0],
                recv_sem.at[slot, piece, k], device_id=partner, device_id_type=MESH).wait_recv()

    def norm_arrived(slot):
        pltpu.make_async_remote_copy(
            norms.at[slot], norms.at[slot], nsend_sem.at[0],
            nrecv_sem.at[slot], device_id=partner, device_id_type=MESH).wait_recv()

    def compute(slot, piece):
        if not COMPUTE:
            return
        j0 = piece * ROWS
        p = buf[slot, 0, pl.ds(j0, ROWS), :]
        v = buf[slot, 1, pl.ds(j0, ROWS), :]
        pp = jnp.concatenate([p, p], axis=1)
        vt = v.T
        v2 = jnp.concatenate([vt, vt], axis=1)
        cols = []
        for q in range(ROWS // 128):
            row = norms[slot, pl.ds(j0 // 128 + q, 1), :]
            cols.append(jnp.broadcast_to(row, (128, 128)).T)
        other = jnp.concatenate(cols, axis=0)
        other = jnp.concatenate([other] * (COLS // 128), axis=1)
        for i in range(0, pts, COLS):
            c = lax.dot_general(pp, left[i:i + COLS, :], (((1,), (1,)), ((), ())),
                                preferred_element_type=jnp.float32)
            k = matern(c, own_sq[0:1, i:i + COLS], other)
            acc[:, i:i + COLS] += jnp.dot(v2, jnp.concatenate(split(k, 2), axis=0),
                                          preferred_element_type=jnp.float32)

    first, second = 3 - core, 2 + core
    if COMM:
        pl.semaphore_wait(barrier, 4)
        send_norm(0, OWN, RIGHT, lower)
        send_norm(1, OWN, LEFT, upper)
        send_norm(2, OWN, PARTNER, partner)
        for piece in range(n_piece):
            send(0, OWN, RIGHT, piece, lower)
            send(1, OWN, LEFT, piece, upper)
            send(2, OWN, PARTNER, piece, partner)

    acc[...] = jnp.zeros_like(acc)

    def both(slot):
        lax.fori_loop(0, n_piece, lambda piece, c: (compute(slot, piece), c)[1], 0)

    both(OWN)
    if not COMM:
        for slot in range(6):
            both(slot)
    if COMM:
        norm_arrived(PARTNER)
        for piece in range(n_piece):
            arrived(PARTNER, piece)
        both(PARTNER)
        norm_arrived(LEFT)
        norm_arrived(RIGHT)
        send_norm(3, LEFT, PLEFT, partner)
        send_norm(4, RIGHT, PRIGHT, partner)
        send_norm(5, first, FAR, outer)
        for piece in range(n_piece):
            arrived(LEFT, piece)
            send(3, LEFT, PLEFT, piece, partner)
            arrived(RIGHT, piece)
            send(4, RIGHT, PRIGHT, piece, partner)
            send(5, first, FAR, piece, outer)
            lax.fori_loop(LEFT, RIGHT + 1, lambda s, c: (compute(s, piece), c)[1], 0)
            if piece == 0:
                norm_arrived(PLEFT)
                norm_arrived(PRIGHT)
            arrived(PLEFT, piece)
            arrived(PRIGHT, piece)
            lax.fori_loop(PLEFT, PRIGHT + 1, lambda s, c: (compute(s, piece), c)[1], 0)
        norm_arrived(FAR)
        for piece in range(n_piece):
            arrived(FAR, piece)
            compute(FAR, piece)

    noise = noise_ref[0]
    for j in range(0, pts, 256):
        o_ref[j:j + 256, :] = acc[:, j:j + 256].T + noise * buf[OWN, 1, j:j + 256, :].astype(jnp.float32)
    for c in sent:
        c.wait_send()


def body(n_lane, n_dev, points, probes, inv_scale, noise_var):
    pts, feats = points.shape
    n_piece = pts // ROWS
    return pl.pallas_call(
        functools.partial(kernel, n_lane, n_dev),
        out_shape=jax.ShapeDtypeStruct((pts, feats), jnp.float32),
        in_specs=[pl.BlockSpec(memory_space=pl.ANY), pl.BlockSpec(memory_space=pl.ANY),
                  pl.BlockSpec(memory_space=pltpu.VMEM), pl.BlockSpec(memory_space=pltpu.SMEM)],
        out_specs=pl.BlockSpec(memory_space=pltpu.VMEM),
        scratch_shapes=[
            pltpu.VMEM((7, 2, pts, feats), jnp.bfloat16),
            pltpu.VMEM((7, 8, 128), jnp.float32),
            pltpu.VMEM((8, pts), jnp.float32),
            pltpu.VMEM((pts, 2 * feats), jnp.bfloat16),
            pltpu.VMEM((feats, pts), jnp.float32),
            pltpu.SemaphoreType.DMA((2,)),
            pltpu.SemaphoreType.DMA((6, n_piece, 2)),
            pltpu.SemaphoreType.DMA((7, n_piece, 2)),
            pltpu.SemaphoreType.DMA((6,)),
            pltpu.SemaphoreType.DMA((7,)),
        ],
        compiler_params=pltpu.CompilerParams(collective_id=0 if COMM else None, has_side_effects=True),
    )(points, probes, inv_scale.reshape(1, feats), noise_var)


def solution(mesh):
    n_lane = mesh.shape["lane"]
    n_dev = n_lane * mesh.shape["blk"]
    in_specs = (P(("blk", "lane"), None), P(("blk", "lane"), None), P(), P())
    return jax.shard_map(functools.partial(body, n_lane, n_dev), mesh=mesh, in_specs=in_specs,
                         out_specs=P(("blk", "lane"), None), check_vma=False)
```

profile of v0, /device:TPU:1, one launch (start us, length us, event | category | flops | bytes accessed | tf_op | source)
XLA Modules:
  0.0 46.8 jit_solution(3972057072350442189)
XLA Ops:
  0.7 44.3 %shard_map.46 = f32[1024,128]{1,0:T(8,128)} custom-call(bf16[1024,128]{1,0:T(8,128)(2,1)} %p_hbm.1, bf16[1024,128]{1,0:T(8,128)(2,1)} %v_hbm.1, f32[1,128]{1,0:T(1,128)} %bitcast.1, f32[1]{0:T(128)S(6)} %copy.6.noise_ref), custom_call_target="tpu_custom_call" | custom-call | tf_op jit(solution)/shard_map/pallas_call | solution.py:190
  44.9 1.9 %copy.7 = f32[1024,128]{1,0:T(8,128)} copy(f32[1024,128]{1,0:T(8,128)} %shard_map.46) | data formatting | bytes 1048576
where the time goes:
time: 47 us; the launch traced here: 46.8 us
  Pallas kernels  44.3 us (94%)
  local copies, waits for them, and re-layouts  1.87 us (4%)
  between operations  0.66 us (1%)
    pallas_call x1, Pallas kernels, body(): pl.pallas_call(functools.partial(kernel, n_lane, n_dev), out_shape=jax.Sh...  44.3 us
    unnamed x1, local copies, waits for them, and re-layouts  1.87 us

commit v1 on v0

v1 whole, which is shorter than its diff:
```python
import functools
import math

import jax
import jax.numpy as jnp
from jax import lax
from jax.experimental import pallas as pl
from jax.experimental.pallas import tpu as pltpu
from jax.sharding import PartitionSpec as P

MESH = pl.DeviceIdType.MESH
LOG2E = math.log2(math.e)
LN2 = math.log(2.0)
SHIFT = math.log2(LN2 * LN2 / 3.0)
LIN = 3.0 / LN2
CON = 3.0 / (LN2 * LN2)
PIECE = 256
ROWS = 512
COLS = 256
RING = 12

OWN, PARTNER, LEFT, RIGHT, PLEFT, PRIGHT, FAR = range(7)
INNER = (((RIGHT, 0), (LEFT, 0), (PRIGHT, 0), (PLEFT, 0), (RIGHT, 1), (LEFT, 1), (PRIGHT, 1), (PLEFT, 1)),
         ((LEFT, 0), (RIGHT, 0), (PLEFT, 0), (PRIGHT, 0), (LEFT, 1), (RIGHT, 1), (PLEFT, 1), (PRIGHT, 1)))
FIRST = ((RIGHT, 0), (PRIGHT, 0), (RIGHT, 1), (PRIGHT, 1), (LEFT, 0), (PLEFT, 0), (LEFT, 1), (PLEFT, 1))


def digits(order, which, base):
    return sum(step[which] * base ** n for n, step in enumerate(order))


def matern(minus_cross, own_sq, other_sq):
    x = jnp.maximum(minus_cross + own_sq + other_sq, 1e-30)
    u = x * lax.rsqrt(x)
    return jnp.exp2(SHIFT - u) * (u * (u + LIN) + CON)


def split(x, parts):
    out = []
    for _ in range(parts):
        piece = x.astype(jnp.bfloat16)
        out.append(piece)
        x = x - piece.astype(jnp.float32)
    return out


def kernel(n_lane, n_dev, p_hbm, v_hbm, scale_ref, o_ref,
           buf, norms, own_sq, left, acc, load_sem, send_sem, recv_sem, nsend_sem, nrecv_sem):
    pts = p_hbm.shape[0]
    n_piece = pts // PIECE
    me = lax.axis_index("blk") * n_lane + lax.axis_index("lane")
    core = lax.rem(me, 2)
    low = 1 - (lax.rem(me // 2, RING) + RING - 1) // RING

    def device(step):
        there = lax.rem(me + step + n_dev, n_dev)
        return (there // n_lane, lax.rem(there, n_lane))

    partner, outer = device(1 - 2 * core), device(2 * core - 1)
    lower, upper = device(-2), device(2)
    inputs = (p_hbm, v_hbm)

    barrier = pltpu.get_barrier_semaphore()
    for there in (partner, outer, lower, upper):
        pl.semaphore_signal(barrier, inc=1, device_id=there, device_id_type=MESH)
    loads = [pltpu.make_async_copy(inputs[k], buf.at[OWN, k], load_sem.at[k]) for k in range(2)]
    for load in loads:
        load.start()

    def copy(flow, src, dst, piece, k, there):
        rows = pl.ds(piece * PIECE, PIECE)
        return pltpu.make_async_remote_copy(
            inputs[k].at[rows] if src is None else buf.at[src, k, rows], buf.at[dst, k, rows],
            send_sem.at[flow, piece, k], recv_sem.at[dst, piece, k],
            device_id=there, device_id_type=MESH)

    def norm_copy(flow, src, dst, there):
        return pltpu.make_async_remote_copy(
            norms.at[src], norms.at[dst], nsend_sem.at[flow], nrecv_sem.at[dst],
            device_id=there, device_id_type=MESH)

    def send(flow, src, dst, piece, there):
        for k in range(2):
            copy(flow, src, dst, piece, k, there).start()

    def arrived(slot, piece):
        for k in range(2):
            copy(0, slot, slot, piece, k, partner).wait_recv()

    pl.semaphore_wait(barrier, 4)
    for piece in range(n_piece):
        send(0, None, RIGHT, piece, lower)
        send(1, None, LEFT, piece, upper)
    for piece in range(n_piece):
        send(2, None, PARTNER, piece, partner)

    loads[0].wait()
    gain = scale_ref[...] * (math.sqrt(5.0) * LOG2E)
    gain = gain * gain
    ones = jnp.ones((8, 384), jnp.bfloat16)
    for j in range(0, pts, 256):
        p = buf[OWN, 0, j:j + 256, :].astype(jnp.float32)
        hi, lo = split(-2.0 * (p * gain), 2)
        left[j:j + 256, 0:128] = hi
        left[j:j + 256, 128:256] = lo
        q = p * (-0.5 * (hi.astype(jnp.float32) + lo.astype(jnp.float32)))
        row = lax.dot_general(ones, jnp.concatenate(split(q, 3), axis=1), (((1,), (1,)), ((), ())),
                              preferred_element_type=jnp.float32)
        own_sq[:, j:j + 256] = row
        norms[OWN, j // 128:j // 128 + 1, :] = row[0:1, 0:128]
        norms[OWN, j // 128 + 1:j // 128 + 2, :] = row[0:1, 128:256]
    loads[1].wait()

    def compute(slot, j0, n_row):
        p = buf[slot, 0, pl.ds(j0, n_row), :]
        v = buf[slot, 1, pl.ds(j0, n_row), :]
        pp = jnp.concatenate([p, p], axis=1)
        vt = v.T
        v2 = jnp.concatenate([vt, vt], axis=1)
        cols = []
        for q in range(n_row // 128):
            row = norms[slot, pl.ds(j0 // 128 + q, 1), :]
            cols.append(jnp.broadcast_to(row, (128, 128)).T)
        other = jnp.concatenate(cols, axis=0)
        other = jnp.concatenate([other] * (COLS // 128), axis=1)
        for i in range(0, pts, COLS):
            c = lax.dot_general(pp, left[i:i + COLS, :], (((1,), (1,)), ((), ())),
                                preferred_element_type=jnp.float32)
            k = matern(c, own_sq[0:1, i:i + COLS], other)
            acc[:, i:i + COLS] += jnp.dot(v2, jnp.concatenate(split(k, 2), axis=0),
                                          preferred_element_type=jnp.float32)

    acc[...] = jnp.zeros_like(acc)

    def near(half, _):
        @pl.when(half == n_half)
        def _():
            norm_copy(0, PARTNER, PARTNER, partner).wait_recv()
            for piece in range(n_piece):
                arrived(PARTNER, piece)

        compute(half // n_half, lax.rem(half, n_half) * ROWS, ROWS)

        @pl.when(half == 0)
        def _():
            norm_copy(0, OWN, RIGHT, lower).start()
            norm_copy(1, OWN, LEFT, upper).start()
            norm_copy(2, OWN, PARTNER, partner).start()
        return 0

    n_half = pts // ROWS
    lax.fori_loop(0, 2 * n_half, near, 0)

    passed_on = 3 - core

    def step(_, codes):
        slots, halves = codes
        slot, half = lax.rem(slots, 8), lax.rem(halves, 2)
        pieces = [half * (ROWS // PIECE) + n for n in range(ROWS // PIECE)]

        @pl.when(half == 0)
        def _():
            norm_copy(0, slot, slot, partner).wait_recv()

            @pl.when(slot < PLEFT)
            def _():
                norm_copy(slot + 1, slot, slot + 2, partner).start()

            @pl.when(slot == passed_on)
            def _():
                norm_copy(5, slot, FAR, outer).start()

        for piece in pieces:
            arrived(slot, piece)

            @pl.when(slot == passed_on)
            def _():
                send(5, slot, FAR, piece, outer)

            @pl.when(slot < PLEFT)
            def _():
                send(slot + 1, slot, slot + 2, piece, partner)

        compute(slot, half * ROWS, ROWS)
        return slots // 8, halves // 2

    slots = low * digits(FIRST, 0, 8) + (1 - low) * (
        (1 - core) * digits(INNER[0], 0, 8) + core * digits(INNER[1], 0, 8))
    halves = low * digits(FIRST, 1, 2) + (1 - low) * digits(INNER[0], 1, 2)
    lax.fori_loop(0, len(FIRST), step, (slots, halves))

    norm_copy(0, FAR, FAR, partner).wait_recv()

    def last(piece, _):
        arrived(FAR, piece)
        compute(FAR, piece * PIECE, PIECE)
        return 0

    lax.fori_loop(0, n_piece, last, 0)

    for j in range(0, pts, 256):
        o_ref[j:j + 256, :] = acc[:, j:j + 256].T
    for flow in range(6):
        norm_copy(flow, OWN, PARTNER, partner).wait_send()
        for piece in range(n_piece):
            for k in range(2):
                copy(flow, OWN, PARTNER, piece, k, partner).wait_send()


def body(n_lane, n_dev, points, probes, inv_scale, noise_var):
    pts, feats = points.shape
    n_piece = pts // PIECE
    product = pl.pallas_call(
        functools.partial(kernel, n_lane, n_dev),
        out_shape=jax.ShapeDtypeStruct((pts, feats), jnp.float32),
        in_specs=[pl.BlockSpec(memory_space=pl.ANY), pl.BlockSpec(memory_space=pl.ANY),
                  pl.BlockSpec(memory_space=pltpu.VMEM)],
        out_specs=pl.BlockSpec(memory_space=pltpu.VMEM),
        scratch_shapes=[
            pltpu.VMEM((7, 2, pts, feats), jnp.bfloat16),
            pltpu.VMEM((7, 8, 128), jnp.float32),
            pltpu.VMEM((8, pts), jnp.float32),
            pltpu.VMEM((pts, 2 * feats), jnp.bfloat16),
            pltpu.VMEM((feats, pts), jnp.float32),
            pltpu.SemaphoreType.DMA((2,)),
            pltpu.SemaphoreType.DMA((6, n_piece, 2)),
            pltpu.SemaphoreType.DMA((7, n_piece, 2)),
            pltpu.SemaphoreType.DMA((6,)),
            pltpu.SemaphoreType.DMA((7,)),
        ],
        compiler_params=pltpu.CompilerParams(collective_id=0, has_side_effects=True),
    )(points, probes, inv_scale.reshape(1, feats))
    return product + noise_var[0] * probes.astype(jnp.float32)


def solution(mesh):
    n_lane = mesh.shape["lane"]
    n_dev = n_lane * mesh.shape["blk"]
    in_specs = (P(("blk", "lane"), None), P(("blk", "lane"), None), P(), P())
    return jax.shard_map(functools.partial(body, n_lane, n_dev), mesh=mesh, in_specs=in_specs,
                         out_specs=P(("blk", "lane"), None), check_vma=False)
```

time: 47 us -> 51.5 us (1.096)
  the two profiles are of different devices: /device:TPU:1 before, /device:TPU:65 now
where the time goes in v1:
time: 51.5 us; the launch traced here: 51.3 us
  Pallas kernels  48.7 us (95%)
  other arithmetic  1.89 us (4%)
  between operations  0.68 us (1%)
    pallas_call x1, Pallas kernels, body(): pl.pallas_call(functools.partial(kernel, n_lane, n_dev), out_shape=jax.Sh...  48.7 us
    add x1, other arithmetic, body(): return product + noise_var[0] * probes.astype(jnp.float32)  1.89 us

profile of v1, /device:TPU:65, one launch (start us, length us, event | category | flops | bytes accessed | tf_op | source)
XLA Modules:
  0.0 51.3 jit_solution(7791123095114555182)
XLA Ops:
  0.7 0.0 copy-start
  0.7 48.7 %shard_map.46 = f32[1024,128]{1,0:T(8,128)} custom-call(bf16[1024,128]{1,0:T(8,128)(2,1)} %p_hbm.1, bf16[1024,128]{1,0:T(8,128)(2,1)} %v_hbm.1, f32[1,128]{1,0:T(1,128)} %bitcast.3), custom_call_target="tpu_custom_call" | custom-call | tf_op jit(solution)/shard_map/pallas_call | solution.py:213
  49.4 0.0 copy-done
  49.4 1.9 %multiply_add_fusion = f32[1024,128]{1,0:T(8,128)} fusion(f32[1024,128]{1,0:T(8,128)} %shard_map.46, bf16[1024,128]{1,0:T(8,128)(2,1)S(1)} %copy-done, f32[]{:T(128)} %bitcast.2), kind=kLoop, calls=%fused_computation | loop fusion | flops 393216 | bytes 1310724 | tf_op jit(solution)/shard_map/add | solution.py:233
Async XLA Ops:
  0.7 48.8 %copy-start = (bf16[1024,128]{1,0:T(8,128)(2,1)S(1)}, bf16[1024,128]{1,0:T(8,128)(2,1)}, u32[]{:S(2)}) copy-start(bf16[1024,128]{1,0:T(8,128)(2,1)} %v_hbm.1) | copy-start | bytes 786436

commit v2 on v1

--- a/solution.py
+++ b/solution.py
@@ -67,11 +67,10 @@
     for load in loads:
         load.start()
 
-    def copy(flow, src, dst, piece, k, there):
+    def copy(flow, src, dst, piece, there):
         rows = pl.ds(piece * PIECE, PIECE)
         return pltpu.make_async_remote_copy(
-            inputs[k].at[rows] if src is None else buf.at[src, k, rows], buf.at[dst, k, rows],
-            send_sem.at[flow, piece, k], recv_sem.at[dst, piece, k],
+            buf.at[src, :, rows], buf.at[dst, :, rows], send_sem.at[flow, piece], recv_sem.at[dst, piece],
             device_id=there, device_id_type=MESH)
 
     def norm_copy(flow, src, dst, there):
@@ -79,22 +78,19 @@
             norms.at[src], norms.at[dst], nsend_sem.at[flow], nrecv_sem.at[dst],
             device_id=there, device_id_type=MESH)
 
-    def send(flow, src, dst, piece, there):
-        for k in range(2):
-            copy(flow, src, dst, piece, k, there).start()
+    def send_own(piece):
+        copy(0, OWN, RIGHT, piece, lower).start()
+        copy(1, OWN, LEFT, piece, upper).start()
+        copy(2, OWN, PARTNER, piece, partner).start()
 
     def arrived(slot, piece):
-        for k in range(2):
-            copy(0, slot, slot, piece, k, partner).wait_recv()
-
+        copy(0, slot, slot, piece, partner).wait_recv()
+
+    for load in loads:
+        load.wait()
     pl.semaphore_wait(barrier, 4)
-    for piece in range(n_piece):
-        send(0, None, RIGHT, piece, lower)
-        send(1, None, LEFT, piece, upper)
-    for piece in range(n_piece):
-        send(2, None, PARTNER, piece, partner)
-
-    loads[0].wait()
+    send_own(0)
+
     gain = scale_ref[...] * (math.sqrt(5.0) * LOG2E)
     gain = gain * gain
     ones = jnp.ones((8, 384), jnp.bfloat16)
@@ -109,7 +105,12 @@
         own_sq[:, j:j + 256] = row
         norms[OWN, j // 128:j // 128 + 1, :] = row[0:1, 0:128]
         norms[OWN, j // 128 + 1:j // 128 + 2, :] = row[0:1, 128:256]
-    loads[1].wait()
+    acc[...] = jnp.zeros_like(acc)
+    norm_copy(0, OWN, RIGHT, lower).start()
+    norm_copy(1, OWN, LEFT, upper).start()
+    norm_copy(2, OWN, PARTNER, partner).start()
+    for piece in range(1, n_piece):
+        send_own(piece)
 
     def compute(slot, j0, n_row):
         p = buf[slot, 0, pl.ds(j0, n_row), :]
@@ -130,8 +131,6 @@
             acc[:, i:i + COLS] += jnp.dot(v2, jnp.concatenate(split(k, 2), axis=0),
                                           preferred_element_type=jnp.float32)
 
-    acc[...] = jnp.zeros_like(acc)
-
     def near(half, _):
         @pl.when(half == n_half)
         def _():
@@ -140,12 +139,6 @@
                 arrived(PARTNER, piece)
 
         compute(half // n_half, lax.rem(half, n_half) * ROWS, ROWS)
-
-        @pl.when(half == 0)
-        def _():
-            norm_copy(0, OWN, RIGHT, lower).start()
-            norm_copy(1, OWN, LEFT, upper).start()
-            norm_copy(2, OWN, PARTNER, partner).start()
         return 0
 
     n_half = pts // ROWS
@@ -153,33 +146,38 @@
 
     passed_on = 3 - core
 
-    def step(_, codes):
+    def step(n, codes):
         slots, halves = codes
         slot, half = lax.rem(slots, 8), lax.rem(halves, 2)
-        pieces = [half * (ROWS // PIECE) + n for n in range(ROWS // PIECE)]
-
-        @pl.when(half == 0)
+
+        for near_slot in (LEFT, RIGHT):
+            for piece in range(n_piece):
+                when_low = 4 * (near_slot == LEFT) + 2 * (piece // 2)
+                when = low * when_low + (1 - low) * (0, 0, 1, 2)[piece]
+
+                @pl.when(n == when)
+                def _():
+                    if piece == 0:
+                        norm_copy(0, near_slot, near_slot, partner).wait_recv()
+                        norm_copy(near_slot + 1, near_slot, near_slot + 2, partner).start()
+                    arrived(near_slot, piece)
+
+                    @pl.when(near_slot == passed_on)
+                    def _():
+                        if piece == 0:
+                            norm_copy(5, near_slot, FAR, outer).start()
+                        copy(5, near_slot, FAR, piece, outer).start()
+
+                    copy(near_slot + 1, near_slot, near_slot + 2, piece, partner).start()
+
+        @pl.when(slot >= PLEFT)
         def _():
-            norm_copy(0, slot, slot, partner).wait_recv()
-
-            @pl.when(slot < PLEFT)
+            @pl.when(half == 0)
             def _():
-                norm_copy(slot + 1, slot, slot + 2, partner).start()
-
-            @pl.when(slot == passed_on)
-            def _():
-                norm_copy(5, slot, FAR, outer).start()
-
-        for piece in pieces:
-            arrived(slot, piece)
-
-            @pl.when(slot == passed_on)
-            def _():
-                send(5, slot, FAR, piece, outer)
-
-            @pl.when(slot < PLEFT)
-            def _():
-                send(slot + 1, slot, slot + 2, piece, partner)
+                norm_copy(0, slot, slot, partner).wait_recv()
+
+            for n_th in range(ROWS // PIECE):
+                arrived(slot, half * (ROWS // PIECE) + n_th)
 
         compute(slot, half * ROWS, ROWS)
         return slots // 8, halves // 2
@@ -203,8 +201,7 @@
     for flow in range(6):
         norm_copy(flow, OWN, PARTNER, partner).wait_send()
         for piece in range(n_piece):
-            for k in range(2):
-                copy(flow, OWN, PARTNER, piece, k, partner).wait_send()
+            copy(flow, OWN, PARTNER, piece, partner).wait_send()
 
 
 def body(n_lane, n_dev, points, probes, inv_scale, noise_var):
@@ -223,8 +220,8 @@
             pltpu.VMEM((pts, 2 * feats), jnp.bfloat16),
             pltpu.VMEM((feats, pts), jnp.float32),
             pltpu.SemaphoreType.DMA((2,)),
-            pltpu.SemaphoreType.DMA((6, n_piece, 2)),
-            pltpu.SemaphoreType.DMA((7, n_piece, 2)),
+            pltpu.SemaphoreType.DMA((6, n_piece)),
+            pltpu.SemaphoreType.DMA((7, n_piece)),
             pltpu.SemaphoreType.DMA((6,)),
             pltpu.SemaphoreType.DMA((7,)),
         ],

time: 51.5 us -> 48.2 us (0.936)
  the two profiles are of different devices: /device:TPU:65 before, /device:TPU:1 now
where the time goes in v2:
time: 48.2 us; the launch traced here: 47.4 us
  Pallas kernels  44.8 us (93%)
  other arithmetic  1.89 us (4%)
  between operations  0.68 us (1%)
    pallas_call x1, Pallas kernels, body(): pl.pallas_call(functools.partial(kernel, n_lane, n_dev), out_shape=jax.Sh...  44.8 us
    add x1, other arithmetic, body(): return product + noise_var[0] * probes.astype(jnp.float32)  1.89 us

profile of v2, /device:TPU:1, one launch (start us, length us, event | category | flops | bytes accessed | tf_op | source)
XLA Modules:
  0.0 47.4 jit_solution(17937188940698578171)
XLA Ops:
  0.7 0.0 copy-start
  0.7 44.8 %shard_map.46 = f32[1024,128]{1,0:T(8,128)} custom-call(bf16[1024,128]{1,0:T(8,128)(2,1)} %p_hbm.1, bf16[1024,128]{1,0:T(8,128)(2,1)} %v_hbm.1, f32[1,128]{1,0:T(1,128)} %bitcast.3), custom_call_target="tpu_custom_call" | custom-call | tf_op jit(solution)/shard_map/pallas_call | solution.py:210
  45.5 0.0 copy-done
  45.5 1.9 %multiply_add_fusion = f32[1024,128]{1,0:T(8,128)} fusion(f32[1024,128]{1,0:T(8,128)} %shard_map.46, bf16[1024,128]{1,0:T(8,128)(2,1)S(1)} %copy-done, f32[]{:T(128)} %bitcast.2), kind=kLoop, calls=%fused_computation | loop fusion | flops 393216 | bytes 1310724 | tf_op jit(solution)/shard_map/add | solution.py:230
Async XLA Ops:
  0.7 44.9 %copy-start = (bf16[1024,128]{1,0:T(8,128)(2,1)S(1)}, bf16[1024,128]{1,0:T(8,128)(2,1)}, u32[]{:S(2)}) copy-start(bf16[1024,128]{1,0:T(8,128)(2,1)} %v_hbm.1) | copy-start | bytes 786436

commit v3 on v2

--- a/solution.py
+++ b/solution.py
@@ -50,7 +50,7 @@
     n_piece = pts // PIECE
     me = lax.axis_index("blk") * n_lane + lax.axis_index("lane")
     core = lax.rem(me, 2)
-    low = 1 - (lax.rem(me // 2, RING) + RING - 1) // RING
+    low = 1 - (lax.rem(me // 2, RING) + RING - 2) // RING
 
     def device(step):
         there = lax.rem(me + step + n_dev, n_dev)

time: 48.2 us -> 47.6 us (0.988); the launches traced: 47.4 us -> 47.4 us
  no operation moved by 1% of the time
where the time goes in v3:
time: 47.6 us; the launch traced here: 47.4 us
  Pallas kernels  44.8 us (94%)
  other arithmetic  1.89 us (4%)
  between operations  0.68 us (1%)
    pallas_call x1, Pallas kernels, body(): pl.pallas_call(functools.partial(kernel, n_lane, n_dev), out_shape=jax.Sh...  44.8 us
    add x1, other arithmetic, body(): return product + noise_var[0] * probes.astype(jnp.float32)  1.89 us

profile of v3, /device:TPU:1, one launch (start us, length us, event | category | flops | bytes accessed | tf_op | source)
XLA Modules:
  0.0 47.4 jit_solution(2274540211588357993)
XLA Ops:
  0.7 0.0 copy-start
  0.7 44.8 %shard_map.46 = f32[1024,128]{1,0:T(8,128)} custom-call(bf16[1024,128]{1,0:T(8,128)(2,1)} %p_hbm.1, bf16[1024,128]{1,0:T(8,128)(2,1)} %v_hbm.1, f32[1,128]{1,0:T(1,128)} %bitcast.3), custom_call_target="tpu_custom_call" | custom-call | tf_op jit(solution)/shard_map/pallas_call | solution.py:210
  45.5 0.0 copy-done
  45.5 1.9 %multiply_add_fusion = f32[1024,128]{1,0:T(8,128)} fusion(f32[1024,128]{1,0:T(8,128)} %shard_map.46, bf16[1024,128]{1,0:T(8,128)(2,1)S(1)} %copy-done, f32[]{:T(128)} %bitcast.2), kind=kLoop, calls=%fused_computation | loop fusion | flops 393216 | bytes 1310724 | tf_op jit(solution)/shard_map/add | solution.py:230
Async XLA Ops:
  0.7 44.9 %copy-start = (bf16[1024,128]{1,0:T(8,128)(2,1)S(1)}, bf16[1024,128]{1,0:T(8,128)(2,1)}, u32[]{:S(2)}) copy-start(bf16[1024,128]{1,0:T(8,128)(2,1)} %v_hbm.1) | copy-start | bytes 786436

commit v4 on v3

--- a/solution.py
+++ b/solution.py
@@ -145,10 +145,26 @@
     lax.fori_loop(0, 2 * n_half, near, 0)
 
     passed_on = 3 - core
+    early = low * core
+
+    def far(n_row):
+        norm_copy(0, FAR, FAR, partner).wait_recv()
+
+        def part(n, _):
+            for n_th in range(n_row // PIECE):
+                arrived(FAR, n * (n_row // PIECE) + n_th)
+            compute(FAR, n * n_row, n_row)
+            return 0
+
+        lax.fori_loop(0, pts // n_row, part, 0)
 
     def step(n, codes):
         slots, halves = codes
         slot, half = lax.rem(slots, 8), lax.rem(halves, 2)
+
+        @pl.when(n == 4 + 8 * (1 - early))
+        def _():
+            far(ROWS)
 
         for near_slot in (LEFT, RIGHT):
             for piece in range(n_piece):
@@ -187,14 +203,9 @@
     halves = low * digits(FIRST, 1, 2) + (1 - low) * digits(INNER[0], 1, 2)
     lax.fori_loop(0, len(FIRST), step, (slots, halves))
 
-    norm_copy(0, FAR, FAR, partner).wait_recv()
-
-    def last(piece, _):
-        arrived(FAR, piece)
-        compute(FAR, piece * PIECE, PIECE)
-        return 0
-
-    lax.fori_loop(0, n_piece, last, 0)
+    @pl.when(early == 0)
+    def _():
+        far(PIECE)
 
     for j in range(0, pts, 256):
         o_ref[j:j + 256, :] = acc[:, j:j + 256].T

time: 47.6 us -> 47.2 us (level)
  Pallas kernels: 44.8 us -> 44.2 us
    pallas_call x1, Pallas kernels: 44.8 us -> 44.2 us  [body(): pl.pallas_call(functools.partial(kernel, n_lane, n_dev), out_shape=jax.Sh...]
where the time goes in v4:
time: 47.2 us; the launch traced here: 46.8 us
  Pallas kernels  44.2 us (94%)
  other arithmetic  1.89 us (4%)
  between operations  0.68 us (1%)
    pallas_call x1, Pallas kernels, body(): pl.pallas_call(functools.partial(kernel, n_lane, n_dev), out_shape=jax.Sh...  44.2 us
    add x1, other arithmetic, body(): return product + noise_var[0] * probes.astype(jnp.float32)  1.89 us

profile of v4, /device:TPU:1, one launch (start us, length us, event | category | flops | bytes accessed | tf_op | source)
XLA Modules:
  0.0 46.8 jit_solution(5854837465736922086)
XLA Ops:
  0.7 0.0 copy-start
  0.7 44.2 %shard_map.46 = f32[1024,128]{1,0:T(8,128)} custom-call(bf16[1024,128]{1,0:T(8,128)(2,1)} %p_hbm.1, bf16[1024,128]{1,0:T(8,128)(2,1)} %v_hbm.1, f32[1,128]{1,0:T(1,128)} %bitcast.3), custom_call_target="tpu_custom_call" | custom-call | tf_op jit(solution)/shard_map/pallas_call | solution.py:221
  44.9 0.0 copy-done
  44.9 1.9 %multiply_add_fusion = f32[1024,128]{1,0:T(8,128)} fusion(f32[1024,128]{1,0:T(8,128)} %shard_map.46, bf16[1024,128]{1,0:T(8,128)(2,1)S(1)} %copy-done, f32[]{:T(128)} %bitcast.2), kind=kLoop, calls=%fused_computation | loop fusion | flops 393216 | bytes 1310724 | tf_op jit(solution)/shard_map/add | solution.py:241
Async XLA Ops:
  0.7 44.2 %copy-start = (bf16[1024,128]{1,0:T(8,128)(2,1)S(1)}, bf16[1024,128]{1,0:T(8,128)(2,1)}, u32[]{:S(2)}) copy-start(bf16[1024,128]{1,0:T(8,128)(2,1)} %v_hbm.1) | copy-start | bytes 786436

commit v5 on v4

--- a/solution.py
+++ b/solution.py
@@ -50,6 +50,7 @@
     n_piece = pts // PIECE
     me = lax.axis_index("blk") * n_lane + lax.axis_index("lane")
     core = lax.rem(me, 2)
+    zero = 1 - (lax.rem(me // 2, RING) + RING - 1) // RING
     low = 1 - (lax.rem(me // 2, RING) + RING - 2) // RING
 
     def device(step):
@@ -86,31 +87,22 @@
     def arrived(slot, piece):
         copy(0, slot, slot, piece, partner).wait_recv()
 
-    for load in loads:
-        load.wait()
-    pl.semaphore_wait(barrier, 4)
-    send_own(0)
-
-    gain = scale_ref[...] * (math.sqrt(5.0) * LOG2E)
-    gain = gain * gain
-    ones = jnp.ones((8, 384), jnp.bfloat16)
-    for j in range(0, pts, 256):
-        p = buf[OWN, 0, j:j + 256, :].astype(jnp.float32)
-        hi, lo = split(-2.0 * (p * gain), 2)
-        left[j:j + 256, 0:128] = hi
-        left[j:j + 256, 128:256] = lo
-        q = p * (-0.5 * (hi.astype(jnp.float32) + lo.astype(jnp.float32)))
-        row = lax.dot_general(ones, jnp.concatenate(split(q, 3), axis=1), (((1,), (1,)), ((), ())),
-                              preferred_element_type=jnp.float32)
-        own_sq[:, j:j + 256] = row
-        norms[OWN, j // 128:j // 128 + 1, :] = row[0:1, 0:128]
-        norms[OWN, j // 128 + 1:j // 128 + 2, :] = row[0:1, 128:256]
-    acc[...] = jnp.zeros_like(acc)
-    norm_copy(0, OWN, RIGHT, lower).start()
-    norm_copy(1, OWN, LEFT, upper).start()
-    norm_copy(2, OWN, PARTNER, partner).start()
-    for piece in range(1, n_piece):
-        send_own(piece)
+    def prepare():
+        gain = scale_ref[...] * (math.sqrt(5.0) * LOG2E)
+        gain = gain * gain
+        ones = jnp.ones((8, 384), jnp.bfloat16)
+        for j in range(0, pts, 256):
+            p = buf[OWN, 0, j:j + 256, :].astype(jnp.float32)
+            hi, lo = split(-2.0 * (p * gain), 2)
+            left[j:j + 256, 0:128] = hi
+            left[j:j + 256, 128:256] = lo
+            q = p * (-0.5 * (hi.astype(jnp.float32) + lo.astype(jnp.float32)))
+            row = lax.dot_general(ones, jnp.concatenate(split(q, 3), axis=1), (((1,), (1,)), ((), ())),
+                                  preferred_element_type=jnp.float32)
+            own_sq[:, j:j + 256] = row
+            norms[OWN, j // 128:j // 128 + 1, :] = row[0:1, 0:128]
+            norms[OWN, j // 128 + 1:j // 128 + 2, :] = row[0:1, 128:256]
+        acc[...] = jnp.zeros_like(acc)
 
     def compute(slot, j0, n_row):
         p = buf[slot, 0, pl.ds(j0, n_row), :]
@@ -131,6 +123,28 @@
             acc[:, i:i + COLS] += jnp.dot(v2, jnp.concatenate(split(k, 2), axis=0),
                                           preferred_element_type=jnp.float32)
 
+    for load in loads:
+        load.wait()
+    n_half = pts // ROWS
+
+    @pl.when(zero == 1)
+    def _():
+        prepare()
+        lax.fori_loop(0, n_half, lambda half, c: (compute(OWN, half * ROWS, ROWS), c)[1], 0)
+
+    pl.semaphore_wait(barrier, 4)
+    send_own(0)
+
+    @pl.when(zero == 0)
+    def _():
+        prepare()
+
+    norm_copy(0, OWN, RIGHT, lower).start()
+    norm_copy(1, OWN, LEFT, upper).start()
+    norm_copy(2, OWN, PARTNER, partner).start()
+    for piece in range(1, n_piece):
+        send_own(piece)
+
     def near(half, _):
         @pl.when(half == n_half)
         def _():
@@ -141,8 +155,7 @@
         compute(half // n_half, lax.rem(half, n_half) * ROWS, ROWS)
         return 0
 
-    n_half = pts // ROWS
-    lax.fori_loop(0, 2 * n_half, near, 0)
+    lax.fori_loop(zero * n_half, 2 * n_half, near, 0)
 
     passed_on = 3 - core
     early = low * core
@@ -162,13 +175,9 @@
         slots, halves = codes
         slot, half = lax.rem(slots, 8), lax.rem(halves, 2)
 
-        @pl.when(n == 4 + 8 * (1 - early))
-        def _():
-            far(ROWS)
-
         for near_slot in (LEFT, RIGHT):
             for piece in range(n_piece):
-                when_low = 4 * (near_slot == LEFT) + 2 * (piece // 2)
+                when_low = 4 + piece // 2 if near_slot == LEFT else 2 * (piece // 2)
                 when = low * when_low + (1 - low) * (0, 0, 1, 2)[piece]
 
                 @pl.when(n == when)
@@ -185,6 +194,10 @@
                         copy(5, near_slot, FAR, piece, outer).start()
 
                     copy(near_slot + 1, near_slot, near_slot + 2, piece, partner).start()
+
+        @pl.when(n == 4 + 8 * (1 - early))
+        def _():
+            far(ROWS)
 
         @pl.when(slot >= PLEFT)
         def _():

time: 47.2 us -> 45.4 us (0.962)
  Pallas kernels: 44.2 us -> 42.7 us
    pallas_call x1, Pallas kernels: 44.2 us -> 42.7 us  [body(): pl.pallas_call(functools.partial(kernel, n_lane, n_dev), out_shape=jax.Sh...]
where the time goes in v5:
time: 45.4 us; the launch traced here: 45.2 us
  Pallas kernels  42.7 us (94%)
  other arithmetic  1.89 us (4%)
  between operations  0.68 us (1%)
    pallas_call x1, Pallas kernels, body(): pl.pallas_call(functools.partial(kernel, n_lane, n_dev), out_shape=jax.Sh...  42.7 us
    add x1, other arithmetic, body(): return product + noise_var[0] * probes.astype(jnp.float32)  1.89 us

profile of v5, /device:TPU:1, one launch (start us, length us, event | category | flops | bytes accessed | tf_op | source)
XLA Modules:
  0.0 45.2 jit_solution(16877295955359226)
XLA Ops:
  0.7 0.0 copy-start
  0.7 42.7 %shard_map.46 = f32[1024,128]{1,0:T(8,128)} custom-call(bf16[1024,128]{1,0:T(8,128)(2,1)} %p_hbm.1, bf16[1024,128]{1,0:T(8,128)(2,1)} %v_hbm.1, f32[1,128]{1,0:T(1,128)} %bitcast.3), custom_call_target="tpu_custom_call" | custom-call | tf_op jit(solution)/shard_map/pallas_call | solution.py:234
  43.3 0.0 copy-done
  43.4 1.9 %multiply_add_fusion = f32[1024,128]{1,0:T(8,128)} fusion(f32[1024,128]{1,0:T(8,128)} %shard_map.46, bf16[1024,128]{1,0:T(8,128)(2,1)S(1)} %copy-done, f32[]{:T(128)} %bitcast.2), kind=kLoop, calls=%fused_computation | loop fusion | flops 393216 | bytes 1310724 | tf_op jit(solution)/shard_map/add | solution.py:254
Async XLA Ops:
  0.7 42.7 %copy-start = (bf16[1024,128]{1,0:T(8,128)(2,1)S(1)}, bf16[1024,128]{1,0:T(8,128)(2,1)}, u32[]{:S(2)}) copy-start(bf16[1024,128]{1,0:T(8,128)(2,1)} %v_hbm.1) | copy-start | bytes 786436

commit v6 on v5

--- a/solution.py
+++ b/solution.py
@@ -51,6 +51,7 @@
     me = lax.axis_index("blk") * n_lane + lax.axis_index("lane")
     core = lax.rem(me, 2)
     zero = 1 - (lax.rem(me // 2, RING) + RING - 1) // RING
+    top = lax.rem(me // 2, RING) // (RING - 1)
     low = 1 - (lax.rem(me // 2, RING) + RING - 2) // RING
 
     def device(step):
@@ -62,8 +63,25 @@
     inputs = (p_hbm, v_hbm)
 
     barrier = pltpu.get_barrier_semaphore()
-    for there in (partner, outer, lower, upper):
-        pl.semaphore_signal(barrier, inc=1, device_id=there, device_id_type=MESH)
+
+    def greet(*devices):
+        for there in devices:
+            pl.semaphore_signal(barrier, inc=1, device_id=there, device_id_type=MESH)
+
+    greet(partner)
+
+    @pl.when(zero == 0)
+    def _():
+        greet(lower)
+
+    @pl.when(top == 0)
+    def _():
+        greet(upper)
+
+    @pl.when(zero * (1 - core) + top * core == 0)
+    def _():
+        greet(outer)
+
     loads = [pltpu.make_async_copy(inputs[k], buf.at[OWN, k], load_sem.at[k]) for k in range(2)]
     for load in loads:
         load.start()
@@ -80,7 +98,10 @@
             device_id=there, device_id_type=MESH)
 
     def send_own(piece):
-        copy(0, OWN, RIGHT, piece, lower).start()
+        @pl.when(zero == 0)
+        def _():
+            copy(0, OWN, RIGHT, piece, lower).start()
+
         copy(1, OWN, LEFT, piece, upper).start()
         copy(2, OWN, PARTNER, piece, partner).start()
 
@@ -132,14 +153,32 @@
         prepare()
         lax.fori_loop(0, n_half, lambda half, c: (compute(OWN, half * ROWS, ROWS), c)[1], 0)
 
-    pl.semaphore_wait(barrier, 4)
+    pl.semaphore_wait(barrier, 4 - zero * (2 - core))
+
+    @pl.when(zero + top == 1)
+    def _():
+        @pl.when(zero == 1)
+        def _():
+            greet(lower)
+
+        @pl.when(top == 1)
+        def _():
+            greet(upper)
+
+        @pl.when(zero * (1 - core) + top * core == 1)
+        def _():
+            greet(outer)
+
     send_own(0)
 
     @pl.when(zero == 0)
     def _():
         prepare()
 
-    norm_copy(0, OWN, RIGHT, lower).start()
+    @pl.when(zero == 0)
+    def _():
+        norm_copy(0, OWN, RIGHT, lower).start()
+
     norm_copy(1, OWN, LEFT, upper).start()
     norm_copy(2, OWN, PARTNER, partner).start()
     for piece in range(1, n_piece):
@@ -174,6 +213,23 @@
     def step(n, codes):
         slots, halves = codes
         slot, half = lax.rem(slots, 8), lax.rem(halves, 2)
+
+        @pl.when(n == 4 + 8 * (1 - early))
+        def _():
+            far(ROWS)
+
+        @pl.when(n == 4 + 8 * (1 - zero))
+        def _():
+            pl.semaphore_wait(barrier, 2 - core)
+            norm_copy(0, OWN, RIGHT, lower).start()
+            for piece in range(n_piece):
+                copy(0, OWN, RIGHT, piece, lower).start()
+
+            @pl.when(core == 0)
+            def _():
+                norm_copy(5, RIGHT, FAR, outer).start()
+                for piece in range(n_piece):
+                    copy(5, RIGHT, FAR, piece, outer).start()
 
         for near_slot in (LEFT, RIGHT):
             for piece in range(n_piece):
@@ -187,17 +243,13 @@
                         norm_copy(near_slot + 1, near_slot, near_slot + 2, partner).start()
                     arrived(near_slot, piece)
 
-                    @pl.when(near_slot == passed_on)
+                    @pl.when(near_slot + 8 * zero * (1 - core) == passed_on)
                     def _():
                         if piece == 0:
                             norm_copy(5, near_slot, FAR, outer).start()
                         copy(5, near_slot, FAR, piece, outer).start()
 
                     copy(near_slot + 1, near_slot, near_slot + 2, piece, partner).start()
-
-        @pl.when(n == 4 + 8 * (1 - early))
-        def _():
-            far(ROWS)
 
         @pl.when(slot >= PLEFT)
         def _():

time: 45.4 us -> 50.5 us (1.11)
  the two profiles are of different devices: /device:TPU:1 before, /device:TPU:2 now
where the time goes in v6:
time: 50.5 us; the launch traced here: 50.3 us
  Pallas kernels  47.7 us (94%)
  other arithmetic  1.89 us (4%)
  between operations  0.68 us (1%)
    pallas_call x1, Pallas kernels, body(): pl.pallas_call(functools.partial(kernel, n_lane, n_dev), out_shape=jax.Sh...  47.7 us
    add x1, other arithmetic, body(): return product + noise_var[0] * probes.astype(jnp.float32)  1.89 us

profile of v6, /device:TPU:2, one launch (start us, length us, event | category | flops | bytes accessed | tf_op | source)
XLA Modules:
  0.0 50.3 jit_solution(15077041075861625379)
XLA Ops:
  0.7 0.0 copy-start
  0.7 47.7 %shard_map.46 = f32[1024,128]{1,0:T(8,128)} custom-call(bf16[1024,128]{1,0:T(8,128)(2,1)} %p_hbm.1, bf16[1024,128]{1,0:T(8,128)(2,1)} %v_hbm.1, f32[1,128]{1,0:T(1,128)} %bitcast.3), custom_call_target="tpu_custom_call" | custom-call | tf_op jit(solution)/shard_map/pallas_call | solution.py:286
  48.4 0.0 copy-done
  48.4 1.9 %multiply_add_fusion = f32[1024,128]{1,0:T(8,128)} fusion(f32[1024,128]{1,0:T(8,128)} %shard_map.46, bf16[1024,128]{1,0:T(8,128)(2,1)S(1)} %copy-done, f32[]{:T(128)} %bitcast.2), kind=kLoop, calls=%fused_computation | loop fusion | flops 393216 | bytes 1310724 | tf_op jit(solution)/shard_map/add | solution.py:306
Async XLA Ops:
  0.7 47.8 %copy-start = (bf16[1024,128]{1,0:T(8,128)(2,1)S(1)}, bf16[1024,128]{1,0:T(8,128)(2,1)}, u32[]{:S(2)}) copy-start(bf16[1024,128]{1,0:T(8,128)(2,1)} %v_hbm.1) | copy-start | bytes 786436

commit v7 on v6

--- a/solution.py
+++ b/solution.py
@@ -23,6 +23,8 @@
 INNER = (((RIGHT, 0), (LEFT, 0), (PRIGHT, 0), (PLEFT, 0), (RIGHT, 1), (LEFT, 1), (PRIGHT, 1), (PLEFT, 1)),
          ((LEFT, 0), (RIGHT, 0), (PLEFT, 0), (PRIGHT, 0), (LEFT, 1), (RIGHT, 1), (PLEFT, 1), (PRIGHT, 1)))
 FIRST = ((RIGHT, 0), (PRIGHT, 0), (RIGHT, 1), (PRIGHT, 1), (LEFT, 0), (PLEFT, 0), (LEFT, 1), (PLEFT, 1))
+
+LAST = ((LEFT, 0), (PLEFT, 0), (LEFT, 1), (PLEFT, 1), (RIGHT, 0), (PRIGHT, 0), (RIGHT, 1), (PRIGHT, 1))
 
 
 def digits(order, which, base):
@@ -148,11 +150,6 @@
         load.wait()
     n_half = pts // ROWS
 
-    @pl.when(zero == 1)
-    def _():
-        prepare()
-        lax.fori_loop(0, n_half, lambda half, c: (compute(OWN, half * ROWS, ROWS), c)[1], 0)
-
     pl.semaphore_wait(barrier, 4 - zero * (2 - core))
 
     @pl.when(zero + top == 1)
@@ -171,9 +168,7 @@
 
     send_own(0)
 
-    @pl.when(zero == 0)
-    def _():
-        prepare()
+    prepare()
 
     @pl.when(zero == 0)
     def _():
@@ -194,7 +189,7 @@
         compute(half // n_half, lax.rem(half, n_half) * ROWS, ROWS)
         return 0
 
-    lax.fori_loop(zero * n_half, 2 * n_half, near, 0)
+    lax.fori_loop(0, 2 * n_half, near, 0)
 
     passed_on = 3 - core
     early = low * core
@@ -234,7 +229,8 @@
         for near_slot in (LEFT, RIGHT):
             for piece in range(n_piece):
                 when_low = 4 + piece // 2 if near_slot == LEFT else 2 * (piece // 2)
-                when = low * when_low + (1 - low) * (0, 0, 1, 2)[piece]
+                when_top = 4 + piece // 2 if near_slot == RIGHT else (0, 0, 1, 2)[piece]
+                when = low * when_low + top * when_top + (1 - low - top) * (0, 0, 1, 2)[piece]
 
                 @pl.when(n == when)
                 def _():
@@ -263,9 +259,9 @@
         compute(slot, half * ROWS, ROWS)
         return slots // 8, halves // 2
 
-    slots = low * digits(FIRST, 0, 8) + (1 - low) * (
+    slots = low * digits(FIRST, 0, 8) + top * digits(LAST, 0, 8) + (1 - low - top) * (
         (1 - core) * digits(INNER[0], 0, 8) + core * digits(INNER[1], 0, 8))
-    halves = low * digits(FIRST, 1, 2) + (1 - low) * digits(INNER[0], 1, 2)
+    halves = (low + top) * digits(FIRST, 1, 2) + (1 - low - top) * digits(INNER[0], 1, 2)
     lax.fori_loop(0, len(FIRST), step, (slots, halves))
 
     @pl.when(early == 0)

time: 50.5 us -> 45.5 us (0.901)
  the two profiles are of different devices: /device:TPU:2 before, /device:TPU:1 now
where the time goes in v7:
time: 45.5 us; the launch traced here: 45.3 us
  Pallas kernels  42.8 us (94%)
  other arithmetic  1.89 us (4%)
  between operations  0.68 us (1%)
    pallas_call x1, Pallas kernels, body(): pl.pallas_call(functools.partial(kernel, n_lane, n_dev), out_shape=jax.Sh...  42.8 us
    add x1, other arithmetic, body(): return product + noise_var[0] * probes.astype(jnp.float32)  1.89 us

profile of v7, /device:TPU:1, one launch (start us, length us, event | category | flops | bytes accessed | tf_op | source)
XLA Modules:
  0.0 45.3 jit_solution(44688540113186979)
XLA Ops:
  0.7 0.0 copy-start
  0.7 42.8 %shard_map.46 = f32[1024,128]{1,0:T(8,128)} custom-call(bf16[1024,128]{1,0:T(8,128)(2,1)} %p_hbm.1, bf16[1024,128]{1,0:T(8,128)(2,1)} %v_hbm.1, f32[1,128]{1,0:T(1,128)} %bitcast.3), custom_call_target="tpu_custom_call" | custom-call | tf_op jit(solution)/shard_map/pallas_call | solution.py:282
  43.4 0.0 copy-done
  43.4 1.9 %multiply_add_fusion = f32[1024,128]{1,0:T(8,128)} fusion(f32[1024,128]{1,0:T(8,128)} %shard_map.46, bf16[1024,128]{1,0:T(8,128)(2,1)S(1)} %copy-done, f32[]{:T(128)} %bitcast.2), kind=kLoop, calls=%fused_computation | loop fusion | flops 393216 | bytes 1310724 | tf_op jit(solution)/shard_map/add | solution.py:302
Async XLA Ops:
  0.7 42.8 %copy-start = (bf16[1024,128]{1,0:T(8,128)(2,1)S(1)}, bf16[1024,128]{1,0:T(8,128)(2,1)}, u32[]{:S(2)}) copy-start(bf16[1024,128]{1,0:T(8,128)(2,1)} %v_hbm.1) | copy-start | bytes 786436

commit v8 on v5

--- a/solution.py
+++ b/solution.py
@@ -205,10 +205,24 @@
             def _():
                 norm_copy(0, slot, slot, partner).wait_recv()
 
-            for n_th in range(ROWS // PIECE):
+            @pl.when(n + early < 8)
+            def _():
+                for n_th in range(ROWS // PIECE):
+                    arrived(slot, half * (ROWS // PIECE) + n_th)
+
+        @pl.when(n + early < 8)
+        def _():
+            compute(slot, half * ROWS, ROWS)
+
+        @pl.when(n + early == 8)
+        def _():
+            def part(n_th, _):
                 arrived(slot, half * (ROWS // PIECE) + n_th)
-
-        compute(slot, half * ROWS, ROWS)
+                compute(slot, half * ROWS + n_th * PIECE, PIECE)
+                return 0
+
+            lax.fori_loop(0, ROWS // PIECE, part, 0)
+
         return slots // 8, halves // 2
 
     slots = low * digits(FIRST, 0, 8) + (1 - low) * (

time: 45.4 us -> 45.9 us (1.011)
  Pallas kernels: 42.7 us -> 43.2 us
    pallas_call x1, Pallas kernels: 42.7 us -> 43.2 us  [body(): pl.pallas_call(functools.partial(kernel, n_lane, n_dev), out_shape=jax.Sh...]
where the time goes in v8:
time: 45.9 us; the launch traced here: 45.7 us
  Pallas kernels  43.2 us (94%)
  other arithmetic  1.89 us (4%)
  between operations  0.68 us (1%)
    pallas_call x1, Pallas kernels, body(): pl.pallas_call(functools.partial(kernel, n_lane, n_dev), out_shape=jax.Sh...  43.2 us
    add x1, other arithmetic, body(): return product + noise_var[0] * probes.astype(jnp.float32)  1.89 us

profile of v8, /device:TPU:1, one launch (start us, length us, event | category | flops | bytes accessed | tf_op | source)
XLA Modules:
  0.0 45.7 jit_solution(11130551217403774984)
XLA Ops:
  0.7 0.0 copy-start
  0.7 43.2 %shard_map.46 = f32[1024,128]{1,0:T(8,128)} custom-call(bf16[1024,128]{1,0:T(8,128)(2,1)} %p_hbm.1, bf16[1024,128]{1,0:T(8,128)(2,1)} %v_hbm.1, f32[1,128]{1,0:T(1,128)} %bitcast.3), custom_call_target="tpu_custom_call" | custom-call | tf_op jit(solution)/shard_map/pallas_call | solution.py:248
  43.8 0.0 copy-done
  43.8 1.9 %multiply_add_fusion = f32[1024,128]{1,0:T(8,128)} fusion(f32[1024,128]{1,0:T(8,128)} %shard_map.46, bf16[1024,128]{1,0:T(8,128)(2,1)S(1)} %copy-done, f32[]{:T(128)} %bitcast.2), kind=kLoop, calls=%fused_computation | loop fusion | flops 393216 | bytes 1310724 | tf_op jit(solution)/shard_map/add | solution.py:268
Async XLA Ops:
  0.7 43.2 %copy-start = (bf16[1024,128]{1,0:T(8,128)(2,1)S(1)}, bf16[1024,128]{1,0:T(8,128)(2,1)}, u32[]{:S(2)}) copy-start(bf16[1024,128]{1,0:T(8,128)(2,1)} %v_hbm.1) | copy-start | bytes 786436
